TPU v7x, 256 devices: a whole 4x4x8 slice. The times are simulated.
256 devices in a mesh: row: 8 (over y, core), col: 32 (over z, x).
Axes of the slice: x: 4, y: 4, z: 8, core: 2. Of those that a mesh axis runs over, the one named last changes fastest.
Arguments:
- ancestor: bfloat16 [16384, 16384], P('row', 'col'), may hold values from -6 to 6, as said below
- panels: bfloat16 [3, 512, 16384], P(None, 'col', 'row'), may hold values from -0.0625 to 0.0625
- diag_inverse: float32 [3, 512, 512], replicated, may hold values from -6 to 6, as said below
- supernode_blocks: int32 [3, 4], replicated, may hold values from 0 to 127, as said below
- row_lists: int32 [3, 64], replicated, may hold values from 0 to 127, as said below
Outputs:
- updated: bfloat16 [16384, 16384], P('row', 'col')
Inputs may be any that keep to these rules, and one draw needn't show every extreme that they name: ancestor is exactly symmetric. `diag_inverse`: each supernode's block is exactly symmetric. `supernode_blocks`: the 3 times 512 / 128 block numbers are all distinct. `row_lists`: each row holds 64 distinct block numbers; row s holds every block of the supernodes before s and none of supernode s or of later ones.
All inputs are finite; a program needn't handle non-finite values.
Results may differ from a plain program's by a relative error of at most 0.002.
Values may be sent and summed in bfloat16 or wider, within the bound.
No kernel may reach another device: no remote copies, remote signals or barrier semaphores. Data moves between devices by JAX's collectives and lax.ppermute only.
A program may use at most 64 MiB of HBM per device.

v0:
```python
import jax
import jax.numpy as jnp
from jax import lax
from jax.sharding import PartitionSpec as P

W = 512
B = 128
S = 3


def spread(value, axis, source):
    kept = jnp.where(lax.axis_index(axis) == source, value, 0).astype(value.dtype)
    return lax.psum(kept, axis)


def block_flags(listed, first_block, block_count):
    block_ids = first_block + jnp.arange(block_count, dtype=jnp.int32)
    return jnp.any(block_ids[:, None] == listed[None, :], axis=1)


def local(ancestor, panels, diag_inverse, supernode_blocks, row_lists):
    row_count = lax.axis_size("row")
    col_count = lax.axis_size("col")
    row_pos = lax.axis_index("row")
    col_pos = lax.axis_index("col")
    local_rows, local_cols = ancestor.shape
    per_node = W // B
    row_blocks = local_rows // B
    col_blocks = local_cols // B
    col_ratio = col_count // row_count
    first_rowblock = row_pos * row_blocks
    first_colblock = col_pos * col_blocks
    current = ancestor
    for supernode in range(S):
        listed = row_lists[supernode]
        owned_blocks = supernode_blocks[supernode]
        row_flags = block_flags(listed, first_rowblock, row_blocks)
        col_flags = block_flags(listed, first_colblock, col_blocks)
        panel_rows = lax.all_gather(panels[supernode], "col", axis=0, tiled=True)
        panel_rows = jnp.where(
            row_flags[None, :, None], panel_rows.reshape(W, row_blocks, B), 0
        ).reshape(W, local_rows)
        partial_value = -lax.dot_general(
            current, panel_rows, (((0,), (1,)), ((), ())), preferred_element_type=jnp.float32
        )
        col_sum = lax.psum(partial_value, "row")
        col_update = (
            jnp.where(col_flags[:, None, None], col_sum.reshape(col_blocks, B, W), 0.0)
            .reshape(local_cols, W)
            .astype(jnp.bfloat16)
        )
        slab_list = [
            spread(col_update, "col", col_ratio * row_pos + shift_idx)
            for shift_idx in range(col_ratio)
        ]
        row_update = jnp.concatenate(slab_list, axis=0)
        cross_part = jnp.dot(panel_rows, row_update, preferred_element_type=jnp.float32)
        cross_term = lax.psum(cross_part.astype(jnp.bfloat16), "row").astype(jnp.float32)
        diag_block = (diag_inverse[supernode] - 0.5 * (cross_term + cross_term.T)).astype(
            jnp.bfloat16
        )
        col_match = (first_colblock + jnp.arange(col_blocks, dtype=jnp.int32))[
            :, None
        ] == owned_blocks[None, :]
        row_match = (first_rowblock + jnp.arange(row_blocks, dtype=jnp.int32))[
            :, None
        ] == owned_blocks[None, :]
        col_hit = jnp.any(col_match, axis=1)
        row_hit = jnp.any(row_match, axis=1)
        col_select = col_match.astype(jnp.bfloat16)
        row_select = row_match.astype(jnp.bfloat16)
        column_fill = jnp.einsum(
            "rkb,jk->rjb",
            row_update.reshape(local_rows, per_node, B),
            col_select,
            preferred_element_type=jnp.float32,
        ).astype(jnp.bfloat16)
        blocks_view = jnp.where(
            col_hit[None, :, None], column_fill, current.reshape(local_rows, col_blocks, B)
        )
        row_fill = jnp.einsum(
            "jkb,ik->ibj",
            col_update.reshape(local_cols, per_node, B),
            row_select,
            preferred_element_type=jnp.float32,
        ).astype(jnp.bfloat16)
        rows_view = jnp.where(
            row_hit[:, None, None], row_fill, blocks_view.reshape(row_blocks, B, local_cols)
        )
        corner = jnp.einsum(
            "ik,kalb,jl->iajb",
            row_select,
            diag_block.reshape(per_node, B, per_node, B),
            col_select,
            preferred_element_type=jnp.float32,
        ).astype(jnp.bfloat16)
        corner_hit = row_hit[:, None, None, None] & col_hit[None, None, :, None]
        grid_view = jnp.where(corner_hit, corner, rows_view.reshape(row_blocks, B, col_blocks, B))
        current = grid_view.reshape(local_rows, local_cols)
    return current


def solution(mesh):
    in_specs = (P("row", "col"), P(None, "col", "row"), P(), P(), P())
    out_specs = P("row", "col")
    return jax.shard_map(local, mesh=mesh, in_specs=in_specs, out_specs=out_specs, check_vma=False)
```

profile of v0, /device:TPU:2, one launch (start us, length us, event | category | flops | bytes accessed | tf_op | source)
XLA Modules:
  0.0 1100.6 jit_solution(17126207968095562700)
XLA Ops:
  9.6 79.9 %all-gather.11.cloned.1.call-done = bf16[1,512,2048]{2,1,0:T(8,128)(2,1)} async-done(((bf16[1,16,2048]{2,1,0:T(8,128)(2,1)}), bf16[1,512,2048]{2,1,0:T(8,128)(2,1)}) %all-gather.11.cloned.1.call-update) | async-done | bytes 2097168 | tf_op jit(solution)/shard_map/all_gather | solution.py:39
  93.0 50.2 %all-reduce.24 = bf16[512,512]{0,1:T(8,128)(2,1)S(1)} all-reduce(f32[512,512]{0,1:T(8,128)S(1)} %fusion.11), channel_id=1, replica_groups=mesh['row'=8,'col'=32] {'row'}, use_global_device_ids=true, to_apply=%region_12.13 | all-reduce | flops 262144 | bytes 1572864 | tf_op jit(solution)/shard_map/psum | solution.py:46
  145.5 152.2 %all-reduce.23.cloned.1.call-done = (bf16[512,512]{0,1:T(8,128)(2,1)}, bf16[512,512]{0,1:T(8,128)(2,1)}, bf16[512,512]{0,1:T(8,128)(2,1)}, bf16[512,512]{0,1:T(8,128)(2,1)}) async-done(((bf16[512,512]{0,1:T(8,128)(2,1)}, bf16[512,512]{0,1:T(8,128)(2,1)}, bf16[512,512]{0,1:T(8,128)(2,1)}, bf16[512,512]{0,1:T(8,128)(2,1)}), (bf16[512,512]{0,1:T(8,128)(2,1)}, bf16[512,512]{0,1:T(8,128)(2,1)}, ...) | async-done | bytes 2097168 | tf_op jit(solution)/shard_map/psum | solution.py:13
  303.0 4.0 reshape.191
  310.4 3.8 bitcast_select_fusion.6
  322.2 5.1 copy.58
  327.3 40.0 %all-reduce.13.cloned.1.call-done = bf16[512,512]{1,0:T(8,128)(2,1)} async-done(((bf16[512,512]{1,0:T(8,128)(2,1)}), bf16[512,512]{1,0:T(8,128)(2,1)}) %all-reduce.13.cloned.1.call-update) | async-done | bytes 524304 | tf_op jit(solution)/shard_map/psum | solution.py:58
  373.5 3.7 copy.59
  377.2 68.5 %all-gather.9.cloned.1.call-done = bf16[1,512,2048]{2,1,0:T(8,128)(2,1)} async-done(((bf16[1,16,2048]{2,1,0:T(8,128)(2,1)}), bf16[1,512,2048]{2,1,0:T(8,128)(2,1)}) %all-gather.9.cloned.1.call-update) | async-done | bytes 2097168 | tf_op jit(solution)/shard_map/all_gather | solution.py:39
  445.7 4.5 fusion.12
  450.2 51.0 %all-reduce.25 = bf16[512,512]{0,1:T(8,128)(2,1)S(1)} all-reduce(f32[512,512]{0,1:T(8,128)} %fusion.12), channel_id=1, replica_groups=mesh['row'=8,'col'=32] {'row'}, use_global_device_ids=true, to_apply=%region_18.19 | all-reduce | flops 262144 | bytes 1572864 | tf_op jit(solution)/shard_map/psum | solution.py:46
  503.4 152.1 %all-reduce.21.cloned.1.call-done = (bf16[512,512]{0,1:T(8,128)(2,1)}, bf16[512,512]{0,1:T(8,128)(2,1)}, bf16[512,512]{0,1:T(8,128)(2,1)}, bf16[512,512]{0,1:T(8,128)(2,1)}) async-done(((bf16[512,512]{0,1:T(8,128)(2,1)}, bf16[512,512]{0,1:T(8,128)(2,1)}, bf16[512,512]{0,1:T(8,128)(2,1)}, bf16[512,512]{0,1:T(8,128)(2,1)}), (bf16[512,512]{0,1:T(8,128)(2,1)}, bf16[512,512]{0,1:T(8,128)(2,1)}, ...) | async-done | bytes 2097168 | tf_op jit(solution)/shard_map/psum | solution.py:13
  664.7 4.4 copy.65
  669.1 5.2 bitcast_select_fusion.3
  674.3 4.1 reshape.223
  684.2 5.1 copy.70
  689.3 37.2 %all-reduce.15.cloned.1.call-done = bf16[512,512]{0,1:T(8,128)(2,1)} async-done(((bf16[512,512]{0,1:T(8,128)(2,1)}), bf16[512,512]{0,1:T(8,128)(2,1)}) %all-reduce.15.cloned.1.call-update) | async-done | bytes 524304 | tf_op jit(solution)/shard_map/psum | solution.py:58
  736.4 68.6 %all-gather.7.cloned.1.call-done = bf16[1,512,2048]{2,1,0:T(8,128)(2,1)} async-done(((bf16[1,16,2048]{2,1,0:T(8,128)(2,1)}), bf16[1,512,2048]{2,1,0:T(8,128)(2,1)}) %all-gather.7.cloned.1.call-update) | async-done | bytes 2097168 | tf_op jit(solution)/shard_map/all_gather | solution.py:39
  805.0 4.5 fusion.15
  809.5 50.8 %all-reduce.26 = bf16[512,512]{0,1:T(8,128)(2,1)S(1)} all-reduce(f32[512,512]{0,1:T(8,128)} %fusion.15), channel_id=1, replica_groups=mesh['row'=8,'col'=32] {'row'}, use_global_device_ids=true, to_apply=%region_24.25 | all-reduce | flops 262144 | bytes 1572864 | tf_op jit(solution)/shard_map/psum | solution.py:46
  865.1 149.7 %all-reduce.19.cloned.1.call-done = (bf16[512,512]{0,1:T(8,128)(2,1)}, bf16[512,512]{0,1:T(8,128)(2,1)}, bf16[512,512]{0,1:T(8,128)(2,1)}, bf16[512,512]{0,1:T(8,128)(2,1)}) async-done(((bf16[512,512]{0,1:T(8,128)(2,1)}, bf16[512,512]{0,1:T(8,128)(2,1)}, bf16[512,512]{0,1:T(8,128)(2,1)}, bf16[512,512]{0,1:T(8,128)(2,1)}), (bf16[512,512]{0,1:T(8,128)(2,1)}, bf16[512,512]{0,1:T(8,128)(2,1)}, ...) | async-done | bytes 2097168 | tf_op jit(solution)/shard_map/psum | solution.py:13
  1022.0 4.5 bitcast_select_fusion
  1034.6 4.2 copy.82
  1038.8 45.6 %all-reduce.17.cloned.1.call-done = bf16[512,512]{0,1:T(8,128)(2,1)} async-done(((bf16[512,512]{0,1:T(8,128)(2,1)}), bf16[512,512]{0,1:T(8,128)(2,1)}) %all-reduce.17.cloned.1.call-update) | async-done | bytes 524304 | tf_op jit(solution)/shard_map/psum | solution.py:58
  (114 shorter events, 87.7 us)
Async XLA Ops:
  6.5 83.0 %all-gather.11.cloned.1.call-start = ((), (), s32[]{:S(2)}) async-start(), calls=%async_computation.5 | async-start | bytes 2162688 | tf_op jit(solution)/shard_map/all_gather | solution.py:39
  8.1 289.5 %all-reduce.23.cloned.1.call-start = ((), (), s32[]{:S(2)}) async-start(), calls=%async_computation.8 | async-start | bytes 4194304 | tf_op jit(solution)/shard_map/psum | solution.py:13
  145.4 222.0 %all-reduce.13.cloned.1.call-start = ((), (), s32[]{:S(2)}) async-start(), calls=%async_computation | async-start | bytes 1048576 | tf_op jit(solution)/shard_map/psum | solution.py:58
  297.6 2.4 copy-start.6
  297.6 2.5 copy-start.4
  297.6 2.5 copy-start.9
  302.3 143.4 %all-gather.9.cloned.1.call-start = ((), (), s32[]{:S(2)}) async-start(), calls=%async_computation.4 | async-start | bytes 2162688 | tf_op jit(solution)/shard_map/all_gather | solution.py:39
  302.9 4.0 copy-start.8
  302.9 352.6 %all-reduce.21.cloned.1.call-start = ((), (), s32[]{:S(2)}) async-start(), calls=%async_computation.7 | async-start | bytes 4194304 | tf_op jit(solution)/shard_map/psum | solution.py:13
  503.4 223.2 %all-reduce.15.cloned.1.call-start = ((), (), s32[]{:S(2)}) async-start(), calls=%async_computation.1 | async-start | bytes 1048576 | tf_op jit(solution)/shard_map/psum | solution.py:58
  655.6 2.4 copy-start.7
  655.6 2.4 copy-start.5
  655.6 3.8 copy-start.10
  658.1 1.3 copy-start
  661.5 143.5 %all-gather.7.cloned.1.call-start = ((), (), s32[]{:S(2)}) async-start(), calls=%async_computation.3 | async-start | bytes 2162688 | tf_op jit(solution)/shard_map/all_gather | solution.py:39
  662.3 352.5 %all-reduce.19.cloned.1.call-start = ((), (), s32[]{:S(2)}) async-start(), calls=%async_computation.6 | async-start | bytes 4194304 | tf_op jit(solution)/shard_map/psum | solution.py:13
  664.7 4.4 copy-start.1
  862.6 221.9 %all-reduce.17.cloned.1.call-start = ((), (), s32[]{:S(2)}) async-start(), calls=%async_computation.2 | async-start | bytes 1048576 | tf_op jit(solution)/shard_map/psum | solution.py:58
  1014.8 2.4 copy-start.3
  1014.8 2.5 copy-start.2
  1014.8 2.5 copy-start.11
Sparse Core Ops, SparseCore 0:
  9.9 79.5 all-gather.10
  145.5 152.0 all-reduce.22
  302.4 64.8 all-reduce.12
  369.8 75.8 all-gather.8
  503.5 152.0 all-reduce.20
  661.6 64.8 all-reduce.14
  729.2 75.8 all-gather.6
  862.7 152.0 all-reduce.18
  1019.6 64.8 all-reduce.16
where the time goes:
time: 1100 us
  waiting for transfers between devices  795 us (72%)
  blocking collectives  152 us (14%)
  local copies, waits for them, and re-layouts  79 us (7%)
  matrix products  47 us (4%)
  between operations  13.6 us (1%)
  other arithmetic  13.1 us (1%)
    psum x3, waiting for transfers between devices, spread(): return lax.psum(kept, axis)  454 us
    all_gather x3, waiting for transfers between devices, local(): panel_rows = lax.all_gather(panels[supernode], 'col', axis=0, tiled=True)  217 us
    psum x3, blocking collectives, local(): col_sum = lax.psum(partial_value, 'row')  152 us
    psum x3, waiting for transfers between devices, local(): lax.psum(cross_part.astype(jnp.bfloat16), 'row').astype(jnp.float32)  123 us
  transfers between devices with their start and end apart: 9, of which 9 were waited for; matrix products, arithmetic and copies ran while one was open for 9% of the time, Pallas kernels for 0%

commit v1 on v0

--- a/solution.py
+++ b/solution.py
@@ -55,7 +55,9 @@
         ]
         row_update = jnp.concatenate(slab_list, axis=0)
         cross_part = jnp.dot(panel_rows, row_update, preferred_element_type=jnp.float32)
-        cross_term = lax.psum(cross_part.astype(jnp.bfloat16), "row").astype(jnp.float32)
+        cross_term = jnp.sum(lax.all_gather(cross_part.astype(jnp.bfloat16), "row"), axis=0).astype(
+            jnp.float32
+        )
         diag_block = (diag_inverse[supernode] - 0.5 * (cross_term + cross_term.T)).astype(
             jnp.bfloat16
         )

time: 1100 us -> 1020 us (0.927)
  waiting for transfers between devices: 795 us -> 680 us
  local copies, waits for them, and re-layouts: 79 us -> 96.8 us
    psum x3 -> x0, waiting for transfers between devices: 123 us -> none  [local(): lax.psum(cross_part.astype(jnp.bfloat16), 'row').astype(jnp.float32)]
  transfers between devices with their start and end apart: 9 -> 9, of which waited for: 9 -> 8; matrix products, arithmetic and copies ran while one was open for 9% -> 11% of each run, Pallas kernels for 0% -> 0%
where the time goes in v1:
time: 1020 us; the launch traced here: 1010 us
  waiting for transfers between devices  680 us (67%)
  blocking collectives  152 us (15%)
  local copies, waits for them, and re-layouts  96.8 us (9%)
  matrix products  49.5 us (5%)
  other arithmetic  19.8 us (2%)
  between operations  13.9 us (1%)
    psum x3, waiting for transfers between devices, spread(): return lax.psum(kept, axis)  456 us
    all_gather x3, waiting for transfers between devices, local(): panel_rows = lax.all_gather(panels[supernode], 'col', axis=0, tiled=True)  216 us
    psum x3, blocking collectives, local(): col_sum = lax.psum(partial_value, 'row')  152 us
    reshape x6, local copies, waits for them, and re-layouts, local(): blocks_view.reshape(row_blocks, B, local_cols)  22.9 us
  transfers between devices with their start and end apart: 9, of which 8 were waited for; matrix products, arithmetic and copies ran while one was open for 11% of the time, Pallas kernels for 0%

profile of v1, /device:TPU:2, one launch (start us, length us, event | category | flops | bytes accessed | tf_op | source)
XLA Modules:
  0.0 1013.6 jit_solution(11961366595848299)
XLA Ops:
  9.6 80.0 %all-gather.17.cloned.1.call-done = bf16[1,512,2048]{2,1,0:T(8,128)(2,1)} async-done(((bf16[1,16,2048]{2,1,0:T(8,128)(2,1)}), bf16[1,512,2048]{2,1,0:T(8,128)(2,1)}) %all-gather.17.cloned.1.call-update) | async-done | bytes 2097168 | tf_op jit(solution)/shard_map/all_gather | solution.py:39
  93.0 50.2 %all-reduce.15 = bf16[512,512]{0,1:T(8,128)(2,1)S(1)} all-reduce(f32[512,512]{0,1:T(8,128)S(1)} %fusion.11), channel_id=1, replica_groups=mesh['row'=8,'col'=32] {'row'}, use_global_device_ids=true, to_apply=%region_12.13 | all-reduce | flops 262144 | bytes 1572864 | tf_op jit(solution)/shard_map/psum | solution.py:46
  145.5 152.1 %all-reduce.14.cloned.1.call-done = (bf16[512,512]{0,1:T(8,128)(2,1)}, bf16[512,512]{0,1:T(8,128)(2,1)}, bf16[512,512]{0,1:T(8,128)(2,1)}, bf16[512,512]{0,1:T(8,128)(2,1)}) async-done(((bf16[512,512]{0,1:T(8,128)(2,1)}, bf16[512,512]{0,1:T(8,128)(2,1)}, bf16[512,512]{0,1:T(8,128)(2,1)}, bf16[512,512]{0,1:T(8,128)(2,1)}), (bf16[512,512]{0,1:T(8,128)(2,1)}, bf16[512,512]{0,1:T(8,128)(2,1)}, ...) | async-done | bytes 2097168 | tf_op jit(solution)/shard_map/psum | solution.py:13
  312.6 4.5 copy.92
  317.0 4.5 bitcast_select_fusion.6
  321.5 4.2 reshape.225
  332.6 5.1 copy.95
  348.7 67.5 %all-gather.15.cloned.1.call-done = bf16[1,512,2048]{2,1,0:T(8,128)(2,1)} async-done(((bf16[1,16,2048]{2,1,0:T(8,128)(2,1)}), bf16[1,512,2048]{2,1,0:T(8,128)(2,1)}) %all-gather.15.cloned.1.call-update) | async-done | bytes 2097168 | tf_op jit(solution)/shard_map/all_gather | solution.py:39
  416.2 4.5 fusion.12
  420.7 50.8 %all-reduce.16 = bf16[512,512]{0,1:T(8,128)(2,1)S(1)} all-reduce(f32[512,512]{0,1:T(8,128)} %fusion.12), channel_id=1, replica_groups=mesh['row'=8,'col'=32] {'row'}, use_global_device_ids=true, to_apply=%region_18.19 | all-reduce | flops 262144 | bytes 1572864 | tf_op jit(solution)/shard_map/psum | solution.py:46
  473.7 152.3 %all-reduce.12.cloned.1.call-done = (bf16[512,512]{0,1:T(8,128)(2,1)}, bf16[512,512]{0,1:T(8,128)(2,1)}, bf16[512,512]{0,1:T(8,128)(2,1)}, bf16[512,512]{0,1:T(8,128)(2,1)}) async-done(((bf16[512,512]{0,1:T(8,128)(2,1)}, bf16[512,512]{0,1:T(8,128)(2,1)}, bf16[512,512]{0,1:T(8,128)(2,1)}, bf16[512,512]{0,1:T(8,128)(2,1)}), (bf16[512,512]{0,1:T(8,128)(2,1)}, bf16[512,512]{0,1:T(8,128)(2,1)}, ...) | async-done | bytes 2097168 | tf_op jit(solution)/shard_map/psum | solution.py:13
  637.9 4.4 copy.102
  642.3 5.4 bitcast_select_fusion.3
  647.6 4.1 reshape.226
  657.6 5.2 copy.107
  676.3 68.2 %all-gather.13.cloned.1.call-done = bf16[1,512,2048]{2,1,0:T(8,128)(2,1)} async-done(((bf16[1,16,2048]{2,1,0:T(8,128)(2,1)}), bf16[1,512,2048]{2,1,0:T(8,128)(2,1)}) %all-gather.13.cloned.1.call-update) | async-done | bytes 2097168 | tf_op jit(solution)/shard_map/all_gather | solution.py:39
  744.6 4.5 fusion.15
  749.1 50.8 %all-reduce.17 = bf16[512,512]{0,1:T(8,128)(2,1)S(1)} all-reduce(f32[512,512]{0,1:T(8,128)} %fusion.15), channel_id=1, replica_groups=mesh['row'=8,'col'=32] {'row'}, use_global_device_ids=true, to_apply=%region_24.25 | all-reduce | flops 262144 | bytes 1572864 | tf_op jit(solution)/shard_map/psum | solution.py:46
  802.3 152.0 %all-reduce.10.cloned.1.call-done = (bf16[512,512]{0,1:T(8,128)(2,1)}, bf16[512,512]{0,1:T(8,128)(2,1)}, bf16[512,512]{0,1:T(8,128)(2,1)}, bf16[512,512]{0,1:T(8,128)(2,1)}) async-done(((bf16[512,512]{0,1:T(8,128)(2,1)}, bf16[512,512]{0,1:T(8,128)(2,1)}, bf16[512,512]{0,1:T(8,128)(2,1)}, bf16[512,512]{0,1:T(8,128)(2,1)}), (bf16[512,512]{0,1:T(8,128)(2,1)}, bf16[512,512]{0,1:T(8,128)(2,1)}, ...) | async-done | bytes 2097168 | tf_op jit(solution)/shard_map/psum | solution.py:13
  965.1 4.4 copy.114
  969.5 5.3 bitcast_select_fusion
  974.9 4.1 reshape.227
  984.8 4.3 copy.119
  989.0 4.6 all-gather.23.cloned.1.call-done
  (136 shorter events, 106.7 us)
Async XLA Ops:
  6.5 83.0 %all-gather.17.cloned.1.call-start = ((), (), s32[]{:S(2)}) async-start(), calls=%async_computation.2 | async-start | bytes 2162688 | tf_op jit(solution)/shard_map/all_gather | solution.py:39
  8.1 289.5 %all-reduce.14.cloned.1.call-start = ((), (), s32[]{:S(2)}) async-start(), calls=%async_computation.8 | async-start | bytes 4194304 | tf_op jit(solution)/shard_map/psum | solution.py:13
  145.5 192.3 %all-gather.19.cloned.1.call-start = ((), (), s32[]{:S(2)}) async-start(), calls=%async_computation.3 | async-start | bytes 4718592 | tf_op jit(solution)/shard_map/all_gather | solution.py:58
  297.6 2.4 copy-start.11
  297.6 2.5 copy-start.8
  297.6 3.9 copy-start.16
  300.2 1.3 copy-start.1
  301.5 3.2 copy-start.4
  303.6 112.5 %all-gather.15.cloned.1.call-start = ((), (), s32[]{:S(2)}) async-start(), calls=%async_computation.1 | async-start | bytes 2162688 | tf_op jit(solution)/shard_map/all_gather | solution.py:39
  304.2 321.8 %all-reduce.12.cloned.1.call-start = ((), (), s32[]{:S(2)}) async-start(), calls=%async_computation.7 | async-start | bytes 4194304 | tf_op jit(solution)/shard_map/psum | solution.py:13
  312.6 4.5 copy-start.5
  473.6 191.7 %all-gather.21.cloned.1.call-start = ((), (), s32[]{:S(2)}) async-start(), calls=%async_computation.4 | async-start | bytes 4718592 | tf_op jit(solution)/shard_map/all_gather | solution.py:58
  626.0 2.4 copy-start.12
  626.0 2.5 copy-start.9
  626.0 3.9 copy-start.15
  631.9 112.6 %all-gather.13.cloned.1.call-start = ((), (), s32[]{:S(2)}) async-start(), calls=%async_computation | async-start | bytes 2162688 | tf_op jit(solution)/shard_map/all_gather | solution.py:39
  632.7 321.6 %all-reduce.10.cloned.1.call-start = ((), (), s32[]{:S(2)}) async-start(), calls=%async_computation.6 | async-start | bytes 4194304 | tf_op jit(solution)/shard_map/psum | solution.py:13
  637.8 4.4 copy-start.6
  665.3 3.4 copy-start
  802.1 191.6 %all-gather.23.cloned.1.call-start = ((), (), s32[]{:S(2)}) async-start(), calls=%async_computation.5 | async-start | bytes 4718592 | tf_op jit(solution)/shard_map/all_gather | solution.py:58
  954.3 2.4 copy-start.13
  954.3 2.5 copy-start.10
  954.3 3.9 copy-start.17
  965.1 4.4 copy-start.7
  (3 other events, 3.4 us)
Sparse Core Ops, SparseCore 0:
  9.9 79.6 all-gather.16
  145.6 151.9 all-reduce.13
  303.8 33.2 all-gather.18
  339.5 76.6 all-gather.14
  473.8 152.1 all-reduce.11
  632.1 33.2 all-gather.20
  667.9 76.6 all-gather.12
  802.2 152.0 all-reduce.9
  960.4 33.2 all-gather.22
